TPU v7x, 32 devices: a whole 2x2x4 slice. The times are simulated.
32 devices in a mesh: snp: 8 (over z, y), samp: 4 (over x, core).
Axes of the slice: x: 2, y: 2, z: 4, core: 2. Of those that a mesh axis runs over, the one named last changes fastest.
Arguments:
- dosage: bfloat16 [5120, 8192], P('samp', 'snp'), may hold values from 0 to 2, as said below
- observed: int32 [5120, 8192], P('samp', 'snp'), may hold values 0 or 1
- band: int32 [8], replicated, may hold values from 1 to 2
Outputs:
- linkage: float32 [8192, 5120], P(('snp', 'samp'))
Inputs may be any that keep to these rules, and one draw needn't show every extreme that they name: `dosage`: real-valued dosages.
All inputs are finite; a program needn't handle non-finite values. No bound on the sum of `observed` on one device may be relied on, other than what follows from the above.
Results may differ from a plain program's by a relative error of at most 0.00055.
Values may be sent and summed in bfloat16 or wider, within the bound.
A program may use at most 128 MiB of HBM per device.

v0:
```python
import jax
import jax.numpy as jnp
from jax import lax
from jax.sharding import PartitionSpec as P

eps = 1e-05


def from_behind(x, axis, by):
    count = lax.axis_size(axis)
    pairs = [(i, i + by) for i in range(count) if 0 <= i + by < count]
    return lax.ppermute(x, axis, pairs)


def pair_kept(band, mine, offset):
    total = band.shape[0]
    other = mine + offset
    inside = (other >= 0) & (other < total)
    other_band = band[jnp.clip(other, 0, total - 1)]
    keep = inside & (abs(offset) <= jnp.minimum(band[mine], other_band))
    return jnp.where(keep, 1.0, 0.0).astype(jnp.float32)


def products(left, right):
    return lax.dot_general(
        left, right, (((0,), (0,)), ((), ())), preferred_element_type=jnp.float32
    )


def on_device(dosage, observed, band):
    width = dosage.shape[1]
    mine = lax.axis_index("snp")
    weight = observed.astype(jnp.float32)
    values = dosage.astype(jnp.float32)
    cnt, first, second = lax.psum(
        (
            jnp.sum(weight, axis=0),
            jnp.sum(weight * values, axis=0),
            jnp.sum(weight * values * values, axis=0),
        ),
        "samp",
    )
    mean = first / cnt
    spread = second - first * mean
    zed = (weight * (values - mean) * lax.rsqrt(spread + eps * cnt)).astype(jnp.bfloat16)
    keeps = [pair_kept(band, mine, offset) for offset in (-2, -1, 0, 1, 2)]
    blocks = []
    for offset in (-2, -1, 0, 1, 2):
        if offset == 0:
            blocks.append(zed)
        else:
            blocks.append(from_behind(zed, "snp", -offset))
    beside_all = jnp.concatenate(blocks, axis=1)
    rows = lax.psum_scatter(products(zed, beside_all), "samp", scatter_dimension=0, tiled=True)
    pieces = [rows[:, k * width : (k + 1) * width] * keeps[k] for k in range(5)]
    linkage = jnp.concatenate(pieces, axis=1)
    return linkage


def solution(mesh):
    return jax.shard_map(
        on_device,
        mesh=mesh,
        in_specs=(P("samp", "snp"), P("samp", "snp"), P()),
        out_specs=P(("snp", "samp"), None),
        check_vma=False,
    )
```

profile of v0, /device:TPU:12, one launch (start us, length us, event | category | flops | bytes accessed | tf_op | source)
XLA Modules:
  0.0 332.3 jit_solution(16635183022785502845)
XLA Ops:
  6.5 4.8 %fusion.4 = (f32[1024]{0:T(1024)S(1)}, f32[1024]{0:T(1024)S(1)}, f32[1024]{0:T(1024)S(1)}) fusion(bf16[1280,1024]{1,0:T(8,128)(2,1)} %param.3, s32[1280,1024]{1,0:T(8,128)} %param.4), kind=kLoop, calls=%fused_computation.8 | loop fusion | flops 9171968 | bytes 7876608 | tf_op jit(solution)/shard_map/reduce_sum | solution.py:38
  11.3 11.2 %all-reduce = (f32[1024]{0:T(1024)S(1)}, f32[1024]{0:T(1024)S(1)}, f32[1024]{0:T(1024)S(1)}) all-reduce(f32[1024]{0:T(1024)S(1)} %get-tuple-element.7, f32[1024]{0:T(1024)S(1)} %get-tuple-element.6, f32[1024]{0:T(1024)S(1)} %get-tuple-element.5), channel_id=1, replica_groups=mesh['snp'=8,'samp'=4] {'samp'}, use_global_device_ids=true, to_apply=%region_3.0 | all-reduce | flops 3072 | bytes 24576 | tf_op jit(solution)/shard_map/psum | solution.py:35
  22.5 3.6 %fusion.2 = bf16[1280,1024]{1,0:T(8,128)(2,1)S(1)} fusion(bf16[1280,1024]{1,0:T(8,128)(2,1)S(1)} %copy-done, s32[1280,1024]{1,0:T(8,128)} %param.4, f32[1024]{0:T(1024)S(1)} %get-tuple-element.11, f32[1024]{0:T(1024)S(1)} %get-tuple-element.12), kind=kLoop, calls=%fused_computation.5 | loop fusion | flops 7864320 | bytes 10493952 | tf_op jit(solution)/shard_map/convert_element_type | solution.py:45
  26.1 3.5 %collective-permute-start = (bf16[1280,1024]{1,0:T(8,128)(2,1)S(1)}, bf16[1280,1024]{1,0:T(8,128)(2,1)S(1)}, u32[]{:S(2)}, u32[]{:S(2)}) collective-permute-start(bf16[1280,1024]{1,0:T(8,128)(2,1)S(1)} %fusion.2), channel_id=1, source_target_pairs={{0,8},{4,12},{8,16},{12,20},{16,24},{20,28},{1,9},{5,13},{9,17},{1... | collective-permute-start | bytes 7864328 | tf_op jit(solution)/shard_map/ppermute | solution.py:12
  29.6 3.4 %collective-permute-start.1 = (bf16[1280,1024]{1,0:T(8,128)(2,1)S(1)}, bf16[1280,1024]{1,0:T(8,128)(2,1)S(1)}, u32[]{:S(2)}, u32[]{:S(2)}) collective-permute-start(bf16[1280,1024]{1,0:T(8,128)(2,1)S(1)} %fusion.2), channel_id=1, source_target_pairs={{0,4},{4,8},{8,12},{12,16},{16,20},{20,24},{24,28},{1,5},{5,9},{9,... | collective-permute-start | bytes 7864328 | tf_op jit(solution)/shard_map/ppermute | solution.py:12
  33.0 2.4 collective-permute-start.2
  35.4 2.7 collective-permute-start.3
  38.1 49.6 %collective-permute-done = bf16[1280,1024]{1,0:T(8,128)(2,1)S(1)} collective-permute-done((bf16[1280,1024]{1,0:T(8,128)(2,1)S(1)}, bf16[1280,1024]{1,0:T(8,128)(2,1)S(1)}, u32[]{:S(2)}, u32[]{:S(2)}) %collective-permute-start) | collective-permute-done | bytes 2621472 | tf_op jit(solution)/shard_map/ppermute | solution.py:12
  87.7 0.2 constant_dynamic-update-slice_fusion.4
  88.0 56.5 %collective-permute-done.1 = bf16[1280,1024]{1,0:T(8,128)(2,1)S(1)} collective-permute-done((bf16[1280,1024]{1,0:T(8,128)(2,1)S(1)}, bf16[1280,1024]{1,0:T(8,128)(2,1)S(1)}, u32[]{:S(2)}, u32[]{:S(2)}) %collective-permute-start.1) | collective-permute-done | bytes 2621472 | tf_op jit(solution)/shard_map/ppermute | solution.py:12
  144.5 0.2 constant_dynamic-update-slice_fusion.3
  144.7 0.2 constant_dynamic-update-slice_fusion.2
  145.0 0.7 collective-permute-done.2
  145.9 0.2 constant_dynamic-update-slice_fusion
  146.2 17.4 %fusion.11 = f32[1024,5120]{1,0:T(8,128)} fusion(bf16[1280,1024]{1,0:T(8,128)(2,1)S(1)} %fusion.2, bf16[1280,5120]{1,0:T(8,128)(2,1)S(1)} %constant_dynamic-update-slice_fusion), kind=kOutput, calls=%fused_computation.26 | convolution fusion | flops 13421772800 | bytes 36700160 | tf_op jit(solution)/shard_map/dot_general | solution.py:25
  163.6 0.6 copy-done.2
  164.2 0.7 fusion.10
  171.6 143.8 %reduce-scatter.2.cloned.1.call-done = f32[256,5120]{1,0:T(8,128)} async-done(((f32[1024,5120]{1,0:T(8,128)}), f32[256,5120]{1,0:T(8,128)}) %reduce-scatter.2.cloned.1.call-update) | async-done | bytes 5242896 | tf_op jit(solution)/shard_map/reduce_scatter | solution.py:54
  315.4 1.3 fusion.9
  316.7 1.3 fusion.8
  318.1 1.3 fusion.7
  319.4 1.3 fusion.6
  320.8 2.3 copy-done.1
  323.1 2.3 fusion.5
  (9 shorter events, 0.3 us)
Async XLA Ops:
  6.5 16.0 %copy-start = (bf16[1280,1024]{1,0:T(8,128)(2,1)S(1)}, bf16[1280,1024]{1,0:T(8,128)(2,1)}, u32[]{:S(2)}) copy-start(bf16[1280,1024]{1,0:T(8,128)(2,1)} %param.3) | copy-start | bytes 7864324
  6.5 308.9 %reduce-scatter.2.cloned.1.call-start = ((), (), s32[]{:S(2)}) async-start(), calls=%async_computation.1 | async-start | bytes 26214400 | tf_op jit(solution)/shard_map/reduce_scatter | solution.py:54
  26.1 61.6 %collective-permute-start = (bf16[1280,1024]{1,0:T(8,128)(2,1)S(1)}, bf16[1280,1024]{1,0:T(8,128)(2,1)S(1)}, u32[]{:S(2)}, u32[]{:S(2)}) collective-permute-start(bf16[1280,1024]{1,0:T(8,128)(2,1)S(1)} %fusion.2), channel_id=1, source_target_pairs={{0,8},{4,12},{8,16},{12,20},{16,24},{20,28},{1,9},{5,13},{9,17},{1... | collective-permute-start | bytes 7864328 | tf_op jit(solution)/shard_map/ppermute | solution.py:12
  29.6 114.9 %collective-permute-start.1 = (bf16[1280,1024]{1,0:T(8,128)(2,1)S(1)}, bf16[1280,1024]{1,0:T(8,128)(2,1)S(1)}, u32[]{:S(2)}, u32[]{:S(2)}) collective-permute-start(bf16[1280,1024]{1,0:T(8,128)(2,1)S(1)} %fusion.2), channel_id=1, source_target_pairs={{0,4},{4,8},{8,12},{12,16},{16,20},{20,24},{24,28},{1,5},{5,9},{9,... | collective-permute-start | bytes 7864328 | tf_op jit(solution)/shard_map/ppermute | solution.py:12
  33.0 112.7 %collective-permute-start.2 = (bf16[1280,1024]{1,0:T(8,128)(2,1)S(1)}, bf16[1280,1024]{1,0:T(8,128)(2,1)S(1)}, u32[]{:S(2)}, u32[]{:S(2)}) collective-permute-start(bf16[1280,1024]{1,0:T(8,128)(2,1)S(1)} %fusion.2), channel_id=1, source_target_pairs={{4,0},{8,4},{12,8},{16,12},{20,16},{24,20},{28,24},{5,1},{9,5},{13... | collective-permute-start | bytes 7864328 | tf_op jit(solution)/shard_map/ppermute | solution.py:12
  35.4 110.5 %collective-permute-start.3 = (bf16[1280,1024]{1,0:T(8,128)(2,1)S(1)}, bf16[1280,1024]{1,0:T(8,128)(2,1)S(1)}, u32[]{:S(2)}, u32[]{:S(2)}) collective-permute-start(bf16[1280,1024]{1,0:T(8,128)(2,1)S(1)} %fusion.2), channel_id=1, source_target_pairs={{8,0},{12,4},{16,8},{20,12},{24,16},{28,20},{9,1},{13,5},{17,9},{2... | collective-permute-start | bytes 7864328 | tf_op jit(solution)/shard_map/ppermute | solution.py:12
  163.6 0.7 copy-start.2
  320.8 2.4 copy-start.1
Sparse Core Ops, SparseCore 0:
  163.7 151.6 reduce-scatter.1
where the time goes:
time: 334 us; the launch traced here: 332 us
  waiting for transfers between devices  251 us (75%)
  between operations  20.3 us (6%)
  matrix products  17.4 us (5%)
  other arithmetic  16 us (5%)
  starting transfers between devices  12 us (4%)
  blocking collectives  11.2 us (3%)
  local copies, waits for them, and re-layouts  4.84 us (1%)
    reduce_scatter x1, waiting for transfers between devices, on_device(): lax.psum_scatter(products(zed, beside_all), 'samp', scatter_dimension=0,...  144 us
    ppermute x4, waiting for transfers between devices, from_behind(): return lax.ppermute(x, axis, pairs)  107 us
    dot_general x1, matrix products, products(): lax.dot_general(left, right, (((0,), (0,)), ((), ())), preferred_element_...  17.4 us
    ppermute x4, starting transfers between devices, from_behind(): return lax.ppermute(x, axis, pairs)  12 us
    psum x1, blocking collectives, on_device(): lax.psum((jnp.sum(weight, axis=0), jnp.sum(weight * values, axis=0), jnp....  11.2 us
  transfers between devices with their start and end apart: 5, of which 4 were waited for; matrix products, arithmetic and copies ran while one was open for 0% of the time, Pallas kernels for 0%

commit v1 on v0

v1 whole, which is shorter than its diff:
```python
import functools

import jax
import jax.numpy as jnp
from jax import lax
from jax.experimental import pallas as pl
from jax.experimental.pallas import tpu as pltpu
from jax.sharding import PartitionSpec as P

eps = 1e-05
MESH = pl.DeviceIdType.MESH
CHUNK = 256


def offset_of(slot, e):
    return jnp.where(slot == 1, -e, jnp.where(slot == 2, -2 * e, jnp.where(slot == 3, 2 * e, jnp.where(slot == 4, e, 0))))


def linkage_kernel(
    nblk, nsamp, nk, band_ref, z_ref, zt_ref, out_ref,
    right, left, acc, part_out, part_in,
    local_sem, out_sem, z_send, z_recv, fwd_send, fwd_recv, relay_send, left_send, left_recv, part_send, part_recv,
):
    b = lax.axis_index("snp")
    s = lax.axis_index("samp")
    ngrp = nsamp // 2
    c = s % 2
    g = s // 2
    mate = s + 1 - 2 * c
    e = 2 * (b % 2) - 1
    width = nk * CHUNK
    nitems = 5 * nk

    def inside(block):
        return (block >= 0) & (block < nblk)

    def has(slot):
        return inside(b + offset_of(slot, e))

    def item(i):
        later = i >= nk
        j = i - nk
        return jnp.where(later, 1 + j % 4, 0), jnp.where(later, j // 4, i)

    barrier = pltpu.get_barrier_semaphore()
    peers = [(b, mate)] + [(b, 2 * ((g + j) % ngrp) + c) for j in range(1, ngrp)]
    for peer in peers:
        pl.semaphore_signal(barrier, inc=1, device_id=peer, device_id_type=MESH)
    for by in (-2, -1, 1, 2):
        @pl.when(inside(b + by))
        def _():
            pl.semaphore_signal(barrier, inc=1, device_id=(b + by, s), device_id_type=MESH)

    def load(k):
        return pltpu.make_async_copy(z_ref.at[:, pl.ds(k * CHUNK, CHUNK)], right.at[0, c, k], local_sem.at[k])

    own_left = pltpu.make_async_copy(zt_ref.at[c], left.at[c], local_sem.at[nk])
    for k in range(nk):
        load(k).start()
    own_left.start()

    beside = [jnp.where(inside(b + by), 1, 0) for by in (-2, -1, 1, 2)]
    pl.semaphore_wait(barrier, len(peers) + sum(beside))

    mate_left = pltpu.make_async_remote_copy(
        zt_ref.at[1 - c], left.at[c], left_send, left_recv, device_id=(b, mate), device_id_type=MESH)
    mate_left_in = pltpu.make_async_remote_copy(
        zt_ref.at[c], left.at[1 - c], left_send, left_recv, device_id=(b, mate), device_id_type=MESH)

    def direct(way, k):
        target = b + (-e, 2 * e, -2 * e)[way - 1]
        return target, pltpu.make_async_remote_copy(
            right.at[0, c, k], right.at[way, c, k], z_send.at[way, k], z_recv.at[way, k],
            device_id=(target, s), device_id_type=MESH)

    def relay(source, target, k):
        return pltpu.make_async_remote_copy(
            right.at[source, c, k], right.at[4, c, k], relay_send.at[k], z_recv.at[4, k],
            device_id=(target, s), device_id_type=MESH)

    def arrival(slot, k):
        return pltpu.make_async_remote_copy(
            right.at[slot, c, k], right.at[slot, c, k], z_send.at[slot, k], z_recv.at[slot, k],
            device_id=(b, mate), device_id_type=MESH)

    def forward(slot, k):
        return pltpu.make_async_remote_copy(
            right.at[slot, c, k], right.at[slot, c, k], fwd_send.at[slot, k], fwd_recv.at[slot, k],
            device_id=(b, mate), device_id_type=MESH)

    def forward_in(slot, k):
        return pltpu.make_async_remote_copy(
            right.at[slot, 1 - c, k], right.at[slot, 1 - c, k], fwd_send.at[slot, k], fwd_recv.at[slot, k],
            device_id=(b, mate), device_id_type=MESH)

    for k in range(nk):
        load(k).wait()
        if k == 0:
            mate_left.start()
        forward(0, k).start()
        for way in (1, 2, 3):
            target, copy = direct(way, k)

            @pl.when(inside(target))
            def _():
                copy.start()
    own_left.wait()

    def receive(i):
        slot, k = item(i)

        @pl.when((slot > 0) & has(slot))
        def _():
            arrival(slot, k).wait_recv()
            forward(slot, k).start()

            @pl.when((slot == 2) & (k % 2 == 0))
            def _():
                relay(2, b - e, k).start()

            @pl.when((slot == 1) & (k % 2 == 1) & has(2))
            def _():
                relay(1, b - 2 * e, k).start()

    def partial(i, j):
        return pltpu.make_async_remote_copy(
            part_out.at[i, j - 1], part_in.at[i, j - 1], part_send.at[i, j - 1], part_recv.at[i, j - 1],
            device_id=(b, 2 * ((g + j) % ngrp) + c), device_id_type=MESH)

    def multiply(i):
        slot, k = item(i)

        @pl.when(has(slot))
        def _():
            forward_in(slot, k).wait_recv()

            def rows(group):
                return jnp.dot(
                    left[0, group], right[slot, 0, k], preferred_element_type=jnp.float32
                ) + jnp.dot(left[1, group], right[slot, 1, k], preferred_element_type=jnp.float32)

            for j in range(1, ngrp):
                part_out[i, j - 1] = rows((g + j) % ngrp)
                partial(i, j).start()
            acc[i] = rows(g)

    mate_left_in.wait_recv()

    def step(i, carry):
        @pl.when(i + 1 < nitems)
        def _():
            receive(i + 1)
        multiply(i)
        return carry

    lax.fori_loop(0, nitems, step, 0)

    def store(i):
        slot, k = item(i)
        column = (offset_of(slot, e) + 2) * width + k * CHUNK
        return pltpu.make_async_copy(acc.at[i], out_ref.at[:, pl.ds(pl.multiple_of(column, CHUNK), CHUNK)], out_sem.at[i])

    def finish(i, carry):
        slot, k = item(i)

        @pl.when(has(slot))
        def _():
            total = acc[i]
            for j in range(1, ngrp):
                partial(i, j).wait_recv()
                total = total + part_in[i, j - 1]
            offset = offset_of(slot, e)
            kept = jnp.abs(offset) <= jnp.minimum(band_ref[b], band_ref[b + offset])
            acc[i] = total * jnp.where(kept, 1.0, 0.0).astype(jnp.float32)

        @pl.when(jnp.logical_not(has(slot)))
        def _():
            acc[i] = jnp.zeros(acc.shape[1:], acc.dtype)
        store(i).start()
        return carry

    lax.fori_loop(0, nitems, finish, 0)

    def drain(i, carry):
        slot, k = item(i)
        store(i).wait()

        @pl.when(has(slot))
        def _():
            forward(slot, k).wait_send()
            for j in range(1, ngrp):
                partial(i, j).wait_send()
        return carry

    lax.fori_loop(0, nitems, drain, 0)
    mate_left.wait_send()
    for k in range(nk):
        for way in (1, 2, 3):
            target, copy = direct(way, k)

            @pl.when(inside(target))
            def _():
                copy.wait_send()

        @pl.when(has(2))
        def _():
            relay(2, b - e, k).wait_send()


def linkage_of(z, zt, band, nblk, nsamp):
    depth, width = z.shape
    nk = width // CHUNK
    ngrp = nsamp // 2
    rows = width // nsamp
    nitems = 5 * nk
    dma = pltpu.SemaphoreType.DMA
    return pl.pallas_call(
        functools.partial(linkage_kernel, nblk, nsamp, nk),
        out_shape=jax.ShapeDtypeStruct((rows, 5 * width), jnp.float32),
        in_specs=[
            pl.BlockSpec(memory_space=pltpu.SMEM),
            pl.BlockSpec(memory_space=pl.ANY),
            pl.BlockSpec(memory_space=pl.ANY),
        ],
        out_specs=pl.BlockSpec(memory_space=pl.ANY),
        scratch_shapes=[
            pltpu.VMEM((5, 2, nk, depth, CHUNK), jnp.bfloat16),
            pltpu.VMEM((2, ngrp, rows, depth), jnp.bfloat16),
            pltpu.VMEM((nitems, rows, CHUNK), jnp.float32),
            pltpu.VMEM((nitems, ngrp - 1, rows, CHUNK), jnp.float32),
            pltpu.VMEM((nitems, ngrp - 1, rows, CHUNK), jnp.float32),
            dma((nk + 1,)),
            dma((nitems,)),
            dma((4, nk)),
            dma((5, nk)),
            dma((5, nk)),
            dma((5, nk)),
            dma((nk,)),
            dma,
            dma,
            dma((nitems, ngrp - 1)),
            dma((nitems, ngrp - 1)),
        ],
        compiler_params=pltpu.CompilerParams(
            collective_id=0, has_side_effects=True, vmem_limit_bytes=60 * 1024 * 1024
        ),
    )(band, z, zt)


def on_device(nblk, nsamp, dosage, observed, band):
    depth, width = dosage.shape
    weight = observed.astype(jnp.float32)
    values = dosage.astype(jnp.float32)
    cnt, first, second = lax.psum(
        (
            jnp.sum(weight, axis=0),
            jnp.sum(weight * values, axis=0),
            jnp.sum(weight * values * values, axis=0),
        ),
        "samp",
    )
    mean = first / cnt
    spread = second - first * mean
    zed = (weight * (values - mean) * lax.rsqrt(spread + eps * cnt)).astype(jnp.bfloat16)
    turned = zed.T.reshape(nsamp // 2, 2, width // nsamp, depth).transpose(1, 0, 2, 3)
    return linkage_of(zed, turned, band, nblk, nsamp)


def solution(mesh):
    return jax.shard_map(
        functools.partial(on_device, mesh.shape["snp"], mesh.shape["samp"]),
        mesh=mesh,
        in_specs=(P("samp", "snp"), P("samp", "snp"), P()),
        out_specs=P(("snp", "samp"), None),
        check_vma=False,
    )
```

time: 334 us -> 188 us (0.56)
  waiting for transfers between devices: 251 us -> 0 us
  Pallas kernels: 0 us -> 154 us
  between operations: 20.3 us -> 0.03 us
  matrix products: 17.4 us -> 0 us
  starting transfers between devices: 12 us -> 0 us
  other arithmetic: 16 us -> 9.02 us
  local copies, waits for them, and re-layouts: 4.84 us -> 11.8 us
    pallas_call x0 -> x1, Pallas kernels: none -> 154 us  [linkage_of(): pl.pallas_call(functools.partial(linkage_kernel, nblk, nsamp, nk), out_sh...]
    reduce_scatter x1 -> x0, waiting for transfers between devices: 144 us -> none  [on_device(): lax.psum_scatter(products(zed, beside_all), 'samp', scatter_dimension=0,...]
    ppermute x4 -> x0, waiting for transfers between devices: 107 us -> none  [from_behind(): return lax.ppermute(x, axis, pairs)]
    dot_general x1 -> x0, matrix products: 17.4 us -> none  [products(): lax.dot_general(left, right, (((0,), (0,)), ((), ())), preferred_element_...]
    ppermute x4 -> x0, starting transfers between devices: 12 us -> none  [from_behind(): return lax.ppermute(x, axis, pairs)]
    unnamed x4 -> x0, other arithmetic: 5.34 us -> none
    reshape x0 -> x1, local copies, waits for them, and re-layouts: none -> 3.41 us  [on_device(): zed.T.reshape(nsamp // 2, 2, width // nsamp, depth).transpose(1, 0, 2, 3)]
  transfers between devices with their start and end apart: 5 -> 0, of which waited for: 4 -> 0; matrix products, arithmetic and copies ran while one was open for 0% -> 0% of each run, Pallas kernels for 0% -> 0%
where the time goes in v1:
time: 188 us; the launch traced here: 186 us
  Pallas kernels  154 us (82%)
  local copies, waits for them, and re-layouts  11.8 us (6%)
  blocking collectives  11.2 us (6%)
  other arithmetic  9.02 us (5%)
    pallas_call x1, Pallas kernels, linkage_of(): pl.pallas_call(functools.partial(linkage_kernel, nblk, nsamp, nk), out_sh...  154 us
    psum x1, blocking collectives, on_device(): lax.psum((jnp.sum(weight, axis=0), jnp.sum(weight * values, axis=0), jnp....  11.2 us
    unnamed x3, local copies, waits for them, and re-layouts  5.42 us
    reduce_sum x1, other arithmetic, on_device(): jnp.sum(weight * values, axis=0)  4.66 us
    convert_element_type x1, other arithmetic, on_device(): (weight * (values - mean) * lax.rsqrt(spread + eps * cnt)).astype(jnp.bfl...  4.35 us

profile of v1, /device:TPU:12, one launch (start us, length us, event | category | flops | bytes accessed | tf_op | source)
XLA Modules:
  0.0 186.4 jit_solution(2069772469642151523)
XLA Ops:
  0.0 4.7 %fusion.4 = (f32[1024]{0:T(1024)S(1)}, f32[1024]{0:T(1024)S(1)}, f32[1024]{0:T(1024)S(1)}) fusion(bf16[1280,1024]{1,0:T(8,128)(2,1)} %param.3, s32[1280,1024]{1,0:T(8,128)} %param.4), kind=kLoop, calls=%fused_computation.8 | loop fusion | flops 9171968 | bytes 7876608 | tf_op jit(solution)/shard_map/reduce_sum | solution.py:257
  4.7 11.2 %all-reduce = (f32[1024]{0:T(1024)S(1)}, f32[1024]{0:T(1024)S(1)}, f32[1024]{0:T(1024)S(1)}) all-reduce(f32[1024]{0:T(1024)S(1)} %get-tuple-element.7, f32[1024]{0:T(1024)S(1)} %get-tuple-element.6, f32[1024]{0:T(1024)S(1)} %get-tuple-element.5), channel_id=1, replica_groups=mesh['snp'=8,'samp'=4] {'samp'}, use_global_device_ids=true, to_apply=%region_3.0 | all-reduce | flops 3072 | bytes 24576 | tf_op jit(solution)/shard_map/psum | solution.py:254
  15.8 4.3 %fusion.2.z_ref = bf16[1280,1024]{1,0:T(8,128)(2,1)S(1)} fusion(bf16[1280,1024]{1,0:T(8,128)(2,1)} %param.3, s32[1280,1024]{1,0:T(8,128)} %param.4, f32[1024]{0:T(1024)S(1)} %get-tuple-element.11, f32[1024]{0:T(1024)S(1)} %get-tuple-element.12), kind=kLoop, calls=%fused_computation.5 | loop fusion | flops 7864320 | bytes 10493952 | tf_op jit(solution)/shard_map/convert_element_type | solution.py:264
  20.2 0.0 copy-start
  20.2 3.0 %copy.4 = bf16[1024,1280]{1,0:T(8,128)(2,1)} copy(bf16[1024,1280]{0,1:T(8,128)(2,1)S(1)} %bitcast.5) | data formatting | bytes 5242880 | tf_op jit(solution)/shard_map/transpose | solution.py:265
  23.2 3.4 %copy.7 = bf16[2,2,256,1280]{3,2,0,1:T(8,128)(2,1)} copy(bf16[2,2,256,1280]{3,2,1,0:T(8,128)(2,1)} %bitcast.6) | data formatting | bytes 5242880 | tf_op jit(solution)/shard_map/reshape | solution.py:265
  26.6 0.0 copy-done
  26.6 154.4 %shard_map.37 = f32[256,5120]{1,0:T(8,128)} custom-call(s32[8]{0:T(128)} %band_ref.1, bf16[1280,1024]{1,0:T(8,128)(2,1)} %copy-done, bf16[2,2,256,1280]{3,2,1,0:T(8,128)(2,1)} %bitcast.7), custom_call_target="tpu_custom_call" | custom-call | tf_op jit(solution)/shard_map/pallas_call | solution.py:217
  181.0 5.4 %copy.9 = f32[256,5120]{1,0:T(8,128)} copy(f32[256,5120]{1,0:T(8,128)} %shard_map.37) | data formatting | bytes 10485760
  (1 shorter events, 0.0 us)
Async XLA Ops:
  20.2 6.4 %copy-start = (bf16[1280,1024]{1,0:T(8,128)(2,1)}, bf16[1280,1024]{1,0:T(8,128)(2,1)S(1)}, u32[]{:S(2)}) copy-start(bf16[1280,1024]{1,0:T(8,128)(2,1)S(1)} %fusion.2.z_ref) | copy-start | bytes 7864324

commit v2 on v1

--- a/solution.py
+++ b/solution.py
@@ -38,9 +38,9 @@
         return inside(b + offset_of(slot, e))
 
     def item(i):
-        later = i >= nk
         j = i - nk
-        return jnp.where(later, 1 + j % 4, 0), jnp.where(later, j // 4, i)
+        slot = jnp.where(i < nk, 0, jnp.where(j < 3 * nk, 1 + j % 3, 4))
+        return slot, jnp.where(i < nk, i, jnp.where(j < 3 * nk, j // 3, j - 3 * nk))
 
     barrier = pltpu.get_barrier_semaphore()
     peers = [(b, mate)] + [(b, 2 * ((g + j) % ngrp) + c) for j in range(1, ngrp)]
@@ -54,7 +54,7 @@
     def load(k):
         return pltpu.make_async_copy(z_ref.at[:, pl.ds(k * CHUNK, CHUNK)], right.at[0, c, k], local_sem.at[k])
 
-    own_left = pltpu.make_async_copy(zt_ref.at[c], left.at[c], local_sem.at[nk])
+    own_left = pltpu.make_async_copy(zt_ref.at[:, c], left.at[c], local_sem.at[nk])
     for k in range(nk):
         load(k).start()
     own_left.start()
@@ -63,9 +63,9 @@
     pl.semaphore_wait(barrier, len(peers) + sum(beside))
 
     mate_left = pltpu.make_async_remote_copy(
-        zt_ref.at[1 - c], left.at[c], left_send, left_recv, device_id=(b, mate), device_id_type=MESH)
+        zt_ref.at[:, 1 - c], left.at[c], left_send, left_recv, device_id=(b, mate), device_id_type=MESH)
     mate_left_in = pltpu.make_async_remote_copy(
-        zt_ref.at[c], left.at[1 - c], left_send, left_recv, device_id=(b, mate), device_id_type=MESH)
+        zt_ref.at[:, c], left.at[1 - c], left_send, left_recv, device_id=(b, mate), device_id_type=MESH)
 
     def direct(way, k):
         target = b + (-e, 2 * e, -2 * e)[way - 1]
@@ -262,7 +262,7 @@
     mean = first / cnt
     spread = second - first * mean
     zed = (weight * (values - mean) * lax.rsqrt(spread + eps * cnt)).astype(jnp.bfloat16)
-    turned = zed.T.reshape(nsamp // 2, 2, width // nsamp, depth).transpose(1, 0, 2, 3)
+    turned = zed.T.reshape(nsamp // 2, 2, width // nsamp, depth)
     return linkage_of(zed, turned, band, nblk, nsamp)
 
 

time: 188 us -> 151 us (0.80)
  Pallas kernels: 154 us -> 122 us
  local copies, waits for them, and re-layouts: 11.8 us -> 8.45 us
    pallas_call x1, Pallas kernels: 154 us -> 122 us  [linkage_of(): pl.pallas_call(functools.partial(linkage_kernel, nblk, nsamp, nk), out_sh...]
    reshape x1 -> x0, local copies, waits for them, and re-layouts: 3.41 us -> none  [on_device(): zed.T.reshape(nsamp // 2, 2, width // nsamp, depth).transpose(1, 0, 2, 3)]
where the time goes in v2:
time: 151 us; the launch traced here: 150 us
  Pallas kernels  122 us (81%)
  blocking collectives  11.2 us (7%)
  other arithmetic  9.02 us (6%)
  local copies, waits for them, and re-layouts  8.45 us (6%)
    pallas_call x1, Pallas kernels, linkage_of(): pl.pallas_call(functools.partial(linkage_kernel, nblk, nsamp, nk), out_sh...  122 us
    psum x1, blocking collectives, on_device(): lax.psum((jnp.sum(weight, axis=0), jnp.sum(weight * values, axis=0), jnp....  11.2 us
    unnamed x3, local copies, waits for them, and re-layouts  5.42 us
    reduce_sum x1, other arithmetic, on_device(): jnp.sum(weight * values, axis=0)  4.66 us
    convert_element_type x1, other arithmetic, on_device(): (weight * (values - mean) * lax.rsqrt(spread + eps * cnt)).astype(jnp.bfl...  4.35 us
    transpose x1, local copies, waits for them, and re-layouts, on_device(): turned = zed.T.reshape(nsamp // 2, 2, width // nsamp, depth)  3.03 us

profile of v2, /device:TPU:12, one launch (start us, length us, event | category | flops | bytes accessed | tf_op | source)
XLA Modules:
  0.0 150.3 jit_solution(8101632510372341037)
XLA Ops:
  0.0 4.7 %fusion.4 = (f32[1024]{0:T(1024)S(1)}, f32[1024]{0:T(1024)S(1)}, f32[1024]{0:T(1024)S(1)}) fusion(bf16[1280,1024]{1,0:T(8,128)(2,1)} %param.3, s32[1280,1024]{1,0:T(8,128)} %param.4), kind=kLoop, calls=%fused_computation.8 | loop fusion | flops 9171968 | bytes 7876608 | tf_op jit(solution)/shard_map/reduce_sum | solution.py:257
  4.7 11.2 %all-reduce = (f32[1024]{0:T(1024)S(1)}, f32[1024]{0:T(1024)S(1)}, f32[1024]{0:T(1024)S(1)}) all-reduce(f32[1024]{0:T(1024)S(1)} %get-tuple-element.7, f32[1024]{0:T(1024)S(1)} %get-tuple-element.6, f32[1024]{0:T(1024)S(1)} %get-tuple-element.5), channel_id=1, replica_groups=mesh['snp'=8,'samp'=4] {'samp'}, use_global_device_ids=true, to_apply=%region_3.0 | all-reduce | flops 3072 | bytes 24576 | tf_op jit(solution)/shard_map/psum | solution.py:254
  15.8 4.3 %fusion.2.z_ref = bf16[1280,1024]{1,0:T(8,128)(2,1)S(1)} fusion(bf16[1280,1024]{1,0:T(8,128)(2,1)} %param.3, s32[1280,1024]{1,0:T(8,128)} %param.4, f32[1024]{0:T(1024)S(1)} %get-tuple-element.11, f32[1024]{0:T(1024)S(1)} %get-tuple-element.12), kind=kLoop, calls=%fused_computation.5 | loop fusion | flops 7864320 | bytes 10493952 | tf_op jit(solution)/shard_map/convert_element_type | solution.py:264
  20.2 0.0 copy-start
  20.2 3.0 %copy.4 = bf16[1024,1280]{1,0:T(8,128)(2,1)} copy(bf16[1024,1280]{0,1:T(8,128)(2,1)S(1)} %bitcast.2) | data formatting | bytes 5242880 | tf_op jit(solution)/shard_map/transpose | solution.py:265
  23.2 0.0 copy-done
  23.2 121.6 %shard_map.37 = f32[256,5120]{1,0:T(8,128)} custom-call(s32[8]{0:T(128)} %band_ref.1, bf16[1280,1024]{1,0:T(8,128)(2,1)} %copy-done, bf16[2,2,256,1280]{3,2,1,0:T(8,128)(2,1)} %bitcast.3), custom_call_target="tpu_custom_call" | custom-call | tf_op jit(solution)/shard_map/pallas_call | solution.py:217
  144.9 5.4 %copy.6 = f32[256,5120]{1,0:T(8,128)} copy(f32[256,5120]{1,0:T(8,128)} %shard_map.37) | data formatting | bytes 10485760
  (1 shorter events, 0.0 us)
Async XLA Ops:
  20.2 3.0 %copy-start = (bf16[1280,1024]{1,0:T(8,128)(2,1)}, bf16[1280,1024]{1,0:T(8,128)(2,1)S(1)}, u32[]{:S(2)}) copy-start(bf16[1280,1024]{1,0:T(8,128)(2,1)S(1)} %fusion.2.z_ref) | copy-start | bytes 7864324

commit v3 on v2

--- a/solution.py
+++ b/solution.py
@@ -17,9 +17,9 @@
 
 
 def linkage_kernel(
-    nblk, nsamp, nk, band_ref, z_ref, zt_ref, out_ref,
-    right, left, acc, part_out, part_in,
-    local_sem, out_sem, z_send, z_recv, fwd_send, fwd_recv, relay_send, left_send, left_recv, part_send, part_recv,
+    nblk, nsamp, nk, band_ref, dosage_ref, observed_ref, out_ref,
+    dosages, marks, stats, right, turned, left_in, acc, part_out, part_in,
+    dosage_sem, mark_sem, stat_send, stat_recv, out_sem, z_send, z_recv, fwd_send, fwd_recv, relay_send, left_send, left_recv, part_send, part_recv,
 ):
     b = lax.axis_index("snp")
     s = lax.axis_index("samp")
@@ -42,30 +42,67 @@
         slot = jnp.where(i < nk, 0, jnp.where(j < 3 * nk, 1 + j % 3, 4))
         return slot, jnp.where(i < nk, i, jnp.where(j < 3 * nk, j // 3, j - 3 * nk))
 
+    def load(k):
+        columns = pl.ds(k * CHUNK, CHUNK)
+        return (
+            pltpu.make_async_copy(dosage_ref.at[:, columns], dosages.at[k], dosage_sem.at[k]),
+            pltpu.make_async_copy(observed_ref.at[:, columns], marks.at[k], mark_sem.at[k]),
+        )
+
+    for k in range(nk):
+        for copy in load(k):
+            copy.start()
+
     barrier = pltpu.get_barrier_semaphore()
-    peers = [(b, mate)] + [(b, 2 * ((g + j) % ngrp) + c) for j in range(1, ngrp)]
-    for peer in peers:
-        pl.semaphore_signal(barrier, inc=1, device_id=peer, device_id_type=MESH)
+    for j in range(1, nsamp):
+        pl.semaphore_signal(barrier, inc=1, device_id=(b, (s + j) % nsamp), device_id_type=MESH)
     for by in (-2, -1, 1, 2):
         @pl.when(inside(b + by))
         def _():
             pl.semaphore_signal(barrier, inc=1, device_id=(b + by, s), device_id_type=MESH)
 
-    def load(k):
-        return pltpu.make_async_copy(z_ref.at[:, pl.ds(k * CHUNK, CHUNK)], right.at[0, c, k], local_sem.at[k])
-
-    own_left = pltpu.make_async_copy(zt_ref.at[:, c], left.at[c], local_sem.at[nk])
-    for k in range(nk):
-        load(k).start()
-    own_left.start()
+    depth = dosages.shape[1]
+    lanes = 128
+
+    for k in range(nk):
+        for copy in load(k):
+            copy.wait()
+
+        def add_rows(r, sums):
+            at = pl.ds(pl.multiple_of(r * lanes, lanes), lanes)
+            weight = marks[k, at, :].astype(jnp.float32)
+            first = weight * dosages[k, at, :].astype(jnp.float32)
+            second = first * dosages[k, at, :].astype(jnp.float32)
+            return tuple(
+                total + jnp.sum(term.reshape(lanes // 8, 8, CHUNK), axis=0)
+                for total, term in zip(sums, (weight, first, second))
+            )
+
+        zero = jnp.zeros((8, CHUNK), jnp.float32)
+        sums = lax.fori_loop(0, depth // lanes, add_rows, (zero, zero, zero))
+        for q in range(3):
+            stats[s, q : q + 1, k * CHUNK : (k + 1) * CHUNK] = jnp.sum(sums[q], axis=0, keepdims=True)
+    stats[s, 3:8, :] = jnp.zeros((5, width), jnp.float32)
 
     beside = [jnp.where(inside(b + by), 1, 0) for by in (-2, -1, 1, 2)]
-    pl.semaphore_wait(barrier, len(peers) + sum(beside))
+    pl.semaphore_wait(barrier, nsamp - 1 + sum(beside))
+
+    def tell(j):
+        return pltpu.make_async_remote_copy(
+            stats.at[s], stats.at[s], stat_send.at[j - 1], stat_recv.at[j - 1],
+            device_id=(b, (s + j) % nsamp), device_id_type=MESH)
+
+    def hear(j):
+        other = (s + nsamp - j) % nsamp
+        return pltpu.make_async_remote_copy(
+            stats.at[other], stats.at[other], stat_send.at[j - 1], stat_recv.at[j - 1],
+            device_id=(b, other), device_id_type=MESH)
+
+    for j in range(1, nsamp):
+        tell(j).start()
 
     mate_left = pltpu.make_async_remote_copy(
-        zt_ref.at[:, 1 - c], left.at[c], left_send, left_recv, device_id=(b, mate), device_id_type=MESH)
-    mate_left_in = pltpu.make_async_remote_copy(
-        zt_ref.at[:, c], left.at[1 - c], left_send, left_recv, device_id=(b, mate), device_id_type=MESH)
+        turned.at[1 - c], left_in, left_send, left_recv, device_id=(b, mate), device_id_type=MESH)
 
     def direct(way, k):
         target = b + (-e, 2 * e, -2 * e)[way - 1]
@@ -93,10 +130,26 @@
             right.at[slot, 1 - c, k], right.at[slot, 1 - c, k], fwd_send.at[slot, k], fwd_recv.at[slot, k],
             device_id=(b, mate), device_id_type=MESH)
 
-    for k in range(nk):
-        load(k).wait()
-        if k == 0:
-            mate_left.start()
+    for j in range(1, nsamp):
+        hear(j).wait_recv()
+    whole = stats[0]
+    for other in range(1, nsamp):
+        whole = whole + stats[other]
+
+    for k in range(nk):
+        part = whole[:, k * CHUNK : (k + 1) * CHUNK]
+        cnt, first, second = part[0:1], part[1:2], part[2:3]
+        mean = first / cnt
+        scale = lax.rsqrt(second - first * mean + eps * cnt)
+
+        def standardize(r, carry):
+            at = pl.ds(pl.multiple_of(r * lanes, lanes), lanes)
+            weight = marks[k, at, :].astype(jnp.float32)
+            values = dosages[k, at, :].astype(jnp.float32)
+            right[0, c, k, at, :] = (weight * (values - mean) * scale).astype(jnp.bfloat16)
+            return carry
+
+        lax.fori_loop(0, depth // lanes, standardize, 0)
         forward(0, k).start()
         for way in (1, 2, 3):
             target, copy = direct(way, k)
@@ -104,7 +157,19 @@
             @pl.when(inside(target))
             def _():
                 copy.start()
-    own_left.wait()
+
+    rows_each = width // nsamp
+    for k in range(nk):
+        def turn(r, carry):
+            at = pl.ds(pl.multiple_of(r * lanes, lanes), lanes)
+            flipped = right[0, c, k, at, :].T
+            for t in range(CHUNK // rows_each):
+                owner = k * (CHUNK // rows_each) + t
+                turned[owner % 2, owner // 2, :, at] = flipped[t * rows_each : (t + 1) * rows_each]
+            return carry
+
+        lax.fori_loop(0, depth // lanes, turn, 0)
+    mate_left.start()
 
     def receive(i):
         slot, k = item(i)
@@ -136,15 +201,15 @@
 
             def rows(group):
                 return jnp.dot(
-                    left[0, group], right[slot, 0, k], preferred_element_type=jnp.float32
-                ) + jnp.dot(left[1, group], right[slot, 1, k], preferred_element_type=jnp.float32)
+                    turned[c, group], right[slot, c, k], preferred_element_type=jnp.float32
+                ) + jnp.dot(left_in[group], right[slot, 1 - c, k], preferred_element_type=jnp.float32)
 
             for j in range(1, ngrp):
                 part_out[i, j - 1] = rows((g + j) % ngrp)
                 partial(i, j).start()
             acc[i] = rows(g)
 
-    mate_left_in.wait_recv()
+    mate_left.wait_recv()
 
     def step(i, carry):
         @pl.when(i + 1 < nitems)
@@ -194,6 +259,8 @@
 
     lax.fori_loop(0, nitems, drain, 0)
     mate_left.wait_send()
+    for j in range(1, nsamp):
+        tell(j).wait_send()
     for k in range(nk):
         for way in (1, 2, 3):
             target, copy = direct(way, k)
@@ -207,8 +274,8 @@
             relay(2, b - e, k).wait_send()
 
 
-def linkage_of(z, zt, band, nblk, nsamp):
-    depth, width = z.shape
+def on_device(nblk, nsamp, dosage, observed, band):
+    depth, width = dosage.shape
     nk = width // CHUNK
     ngrp = nsamp // 2
     rows = width // nsamp
@@ -224,12 +291,19 @@
         ],
         out_specs=pl.BlockSpec(memory_space=pl.ANY),
         scratch_shapes=[
+            pltpu.VMEM((nk, depth, CHUNK), jnp.bfloat16),
+            pltpu.VMEM((nk, depth, CHUNK), jnp.int32),
+            pltpu.VMEM((nsamp, 8, width), jnp.float32),
             pltpu.VMEM((5, 2, nk, depth, CHUNK), jnp.bfloat16),
             pltpu.VMEM((2, ngrp, rows, depth), jnp.bfloat16),
+            pltpu.VMEM((ngrp, rows, depth), jnp.bfloat16),
             pltpu.VMEM((nitems, rows, CHUNK), jnp.float32),
             pltpu.VMEM((nitems, ngrp - 1, rows, CHUNK), jnp.float32),
             pltpu.VMEM((nitems, ngrp - 1, rows, CHUNK), jnp.float32),
-            dma((nk + 1,)),
+            dma((nk,)),
+            dma((nk,)),
+            dma((nsamp - 1,)),
+            dma((nsamp - 1,)),
             dma((nitems,)),
             dma((4, nk)),
             dma((5, nk)),
@@ -244,26 +318,7 @@
         compiler_params=pltpu.CompilerParams(
             collective_id=0, has_side_effects=True, vmem_limit_bytes=60 * 1024 * 1024
         ),
-    )(band, z, zt)
-
-
-def on_device(nblk, nsamp, dosage, observed, band):
-    depth, width = dosage.shape
-    weight = observed.astype(jnp.float32)
-    values = dosage.astype(jnp.float32)
-    cnt, first, second = lax.psum(
-        (
-            jnp.sum(weight, axis=0),
-            jnp.sum(weight * values, axis=0),
-            jnp.sum(weight * values * values, axis=0),
-        ),
-        "samp",
-    )
-    mean = first / cnt
-    spread = second - first * mean
-    zed = (weight * (values - mean) * lax.rsqrt(spread + eps * cnt)).astype(jnp.bfloat16)
-    turned = zed.T.reshape(nsamp // 2, 2, width // nsamp, depth)
-    return linkage_of(zed, turned, band, nblk, nsamp)
+    )(band, dosage, observed)
 
 
 def solution(mesh):

time: 151 us -> 137 us (0.907)
  blocking collectives: 11.2 us -> 0 us
  Pallas kernels: 122 us -> 132 us
  other arithmetic: 9.02 us -> 0 us
  local copies, waits for them, and re-layouts: 8.45 us -> 5.41 us
    psum x1 -> x0, blocking collectives: 11.2 us -> none  [on_device(): lax.psum((jnp.sum(weight, axis=0), jnp.sum(weight * values, axis=0), jnp....]
    pallas_call x1, Pallas kernels: 122 us -> 132 us  [on_device(): pl.pallas_call(functools.partial(linkage_kernel, nblk, nsamp, nk), out_sh...]
    reduce_sum x1 -> x0, other arithmetic: 4.66 us -> none  [on_device(): jnp.sum(weight * values, axis=0)]
    convert_element_type x1 -> x0, other arithmetic: 4.35 us -> none  [on_device(): (weight * (values - mean) * lax.rsqrt(spread + eps * cnt)).astype(jnp.bfl...]
    transpose x1 -> x0, local copies, waits for them, and re-layouts: 3.03 us -> none  [on_device(): turned = zed.T.reshape(nsamp // 2, 2, width // nsamp, depth)]
    unnamed x3 -> x1, local copies, waits for them, and re-layouts: 5.42 us -> 5.41 us
where the time goes in v3:
time: 137 us
  Pallas kernels  132 us (96%)
  local copies, waits for them, and re-layouts  5.41 us (4%)
    pallas_call x1, Pallas kernels, on_device(): pl.pallas_call(functools.partial(linkage_kernel, nblk, nsamp, nk), out_sh...  132 us
    unnamed x1, local copies, waits for them, and re-layouts  5.41 us

profile of v3, /device:TPU:12, one launch (start us, length us, event | category | flops | bytes accessed | tf_op | source)
XLA Modules:
  0.0 137.1 jit_solution(14983336821732626093)
XLA Ops:
  0.0 131.6 %shard_map.37 = f32[256,5120]{1,0:T(8,128)} custom-call(s32[8]{0:T(128)} %band_ref.1, bf16[1280,1024]{1,0:T(8,128)(2,1)} %dosage_ref.1, s32[1280,1024]{1,0:T(8,128)} %observed_ref.1), custom_call_target="tpu_custom_call" | custom-call | tf_op jit(solution)/shard_map/pallas_call | solution.py:284
  131.6 5.4 %copy.5 = f32[256,5120]{1,0:T(8,128)} copy(f32[256,5120]{1,0:T(8,128)} %shard_map.37) | data formatting | bytes 10485760

commit v4 on v3

--- a/solution.py
+++ b/solution.py
@@ -101,8 +101,10 @@
     for j in range(1, nsamp):
         tell(j).start()
 
-    mate_left = pltpu.make_async_remote_copy(
-        turned.at[1 - c], left_in, left_send, left_recv, device_id=(b, mate), device_id_type=MESH)
+    def mate_left(group):
+        return pltpu.make_async_remote_copy(
+            turned.at[1 - c, group], left_in.at[group], left_send.at[group], left_recv.at[group],
+            device_id=(b, mate), device_id_type=MESH)
 
     def direct(way, k):
         target = b + (-e, 2 * e, -2 * e)[way - 1]
@@ -136,6 +138,8 @@
     for other in range(1, nsamp):
         whole = whole + stats[other]
 
+    rows_each = width // nsamp
+    each = CHUNK // rows_each
     for k in range(nk):
         part = whole[:, k * CHUNK : (k + 1) * CHUNK]
         cnt, first, second = part[0:1], part[1:2], part[2:3]
@@ -146,11 +150,19 @@
             at = pl.ds(pl.multiple_of(r * lanes, lanes), lanes)
             weight = marks[k, at, :].astype(jnp.float32)
             values = dosages[k, at, :].astype(jnp.float32)
-            right[0, c, k, at, :] = (weight * (values - mean) * scale).astype(jnp.bfloat16)
+            zed = (weight * (values - mean) * scale).astype(jnp.bfloat16)
+            right[0, c, k, at, :] = zed
+            flipped = zed.T
+            for t in range(each):
+                owner = k * each + t
+                turned[owner % 2, owner // 2, :, at] = flipped[t * rows_each : (t + 1) * rows_each]
             return carry
 
         lax.fori_loop(0, depth // lanes, standardize, 0)
-        forward(0, k).start()
+        if k == 0:
+            forward(0, k).start()
+        for group in range(k * each // 2, (k + 1) * each // 2):
+            mate_left(group).start()
         for way in (1, 2, 3):
             target, copy = direct(way, k)
 
@@ -158,18 +170,8 @@
             def _():
                 copy.start()
 
-    rows_each = width // nsamp
-    for k in range(nk):
-        def turn(r, carry):
-            at = pl.ds(pl.multiple_of(r * lanes, lanes), lanes)
-            flipped = right[0, c, k, at, :].T
-            for t in range(CHUNK // rows_each):
-                owner = k * (CHUNK // rows_each) + t
-                turned[owner % 2, owner // 2, :, at] = flipped[t * rows_each : (t + 1) * rows_each]
-            return carry
-
-        lax.fori_loop(0, depth // lanes, turn, 0)
-    mate_left.start()
+    for k in range(1, nk):
+        forward(0, k).start()
 
     def receive(i):
         slot, k = item(i)
@@ -209,7 +211,8 @@
                 partial(i, j).start()
             acc[i] = rows(g)
 
-    mate_left.wait_recv()
+    for group in range(ngrp):
+        mate_left(group).wait_recv()
 
     def step(i, carry):
         @pl.when(i + 1 < nitems)
@@ -258,7 +261,8 @@
         return carry
 
     lax.fori_loop(0, nitems, drain, 0)
-    mate_left.wait_send()
+    for group in range(ngrp):
+        mate_left(group).wait_send()
     for j in range(1, nsamp):
         tell(j).wait_send()
     for k in range(nk):
@@ -310,8 +314,8 @@
             dma((5, nk)),
             dma((5, nk)),
             dma((nk,)),
-            dma,
-            dma,
+            dma((ngrp,)),
+            dma((ngrp,)),
             dma((nitems, ngrp - 1)),
             dma((nitems, ngrp - 1)),
         ],

time: 137 us -> 136 us (level)
  Pallas kernels: 132 us -> 130 us
    pallas_call x1, Pallas kernels: 132 us -> 130 us  [on_device(): pl.pallas_call(functools.partial(linkage_kernel, nblk, nsamp, nk), out_sh...]
where the time goes in v4:
time: 136 us
  Pallas kernels  130 us (96%)
  local copies, waits for them, and re-layouts  5.41 us (4%)
    pallas_call x1, Pallas kernels, on_device(): pl.pallas_call(functools.partial(linkage_kernel, nblk, nsamp, nk), out_sh...  130 us
    unnamed x1, local copies, waits for them, and re-layouts  5.41 us

profile of v4, /device:TPU:12, one launch (start us, length us, event | category | flops | bytes accessed | tf_op | source)
XLA Modules:
  0.0 135.5 jit_solution(11992424184586974567)
XLA Ops:
  0.0 130.1 %shard_map.37 = f32[256,5120]{1,0:T(8,128)} custom-call(s32[8]{0:T(128)} %band_ref.1, bf16[1280,1024]{1,0:T(8,128)(2,1)} %dosage_ref.1, s32[1280,1024]{1,0:T(8,128)} %observed_ref.1), custom_call_target="tpu_custom_call" | custom-call | tf_op jit(solution)/shard_map/pallas_call | solution.py:288
  130.1 5.4 %copy.5 = f32[256,5120]{1,0:T(8,128)} copy(f32[256,5120]{1,0:T(8,128)} %shard_map.37) | data formatting | bytes 10485760

commit v5 on v4

--- a/solution.py
+++ b/solution.py
@@ -64,6 +64,17 @@
     depth = dosages.shape[1]
     lanes = 128
 
+    def tell(j, k):
+        return pltpu.make_async_remote_copy(
+            stats.at[s, k], stats.at[s, k], stat_send.at[j - 1, k], stat_recv.at[j - 1, k],
+            device_id=(b, (s + j) % nsamp), device_id_type=MESH)
+
+    def hear(j, k):
+        other = (s + nsamp - j) % nsamp
+        return pltpu.make_async_remote_copy(
+            stats.at[other, k], stats.at[other, k], stat_send.at[j - 1, k], stat_recv.at[j - 1, k],
+            device_id=(b, other), device_id_type=MESH)
+
     for k in range(nk):
         for copy in load(k):
             copy.wait()
@@ -81,25 +92,13 @@
         zero = jnp.zeros((8, CHUNK), jnp.float32)
         sums = lax.fori_loop(0, depth // lanes, add_rows, (zero, zero, zero))
         for q in range(3):
-            stats[s, q : q + 1, k * CHUNK : (k + 1) * CHUNK] = jnp.sum(sums[q], axis=0, keepdims=True)
-    stats[s, 3:8, :] = jnp.zeros((5, width), jnp.float32)
-
-    beside = [jnp.where(inside(b + by), 1, 0) for by in (-2, -1, 1, 2)]
-    pl.semaphore_wait(barrier, nsamp - 1 + sum(beside))
-
-    def tell(j):
-        return pltpu.make_async_remote_copy(
-            stats.at[s], stats.at[s], stat_send.at[j - 1], stat_recv.at[j - 1],
-            device_id=(b, (s + j) % nsamp), device_id_type=MESH)
-
-    def hear(j):
-        other = (s + nsamp - j) % nsamp
-        return pltpu.make_async_remote_copy(
-            stats.at[other], stats.at[other], stat_send.at[j - 1], stat_recv.at[j - 1],
-            device_id=(b, other), device_id_type=MESH)
-
-    for j in range(1, nsamp):
-        tell(j).start()
+            stats[s, k, q : q + 1, :] = jnp.sum(sums[q], axis=0, keepdims=True)
+        stats[s, k, 3:8, :] = jnp.zeros((5, CHUNK), jnp.float32)
+        if k == 0:
+            beside = [jnp.where(inside(b + by), 1, 0) for by in (-2, -1, 1, 2)]
+            pl.semaphore_wait(barrier, nsamp - 1 + sum(beside))
+        for j in range(1, nsamp):
+            tell(j, k).start()
 
     def mate_left(group):
         return pltpu.make_async_remote_copy(
@@ -132,16 +131,14 @@
             right.at[slot, 1 - c, k], right.at[slot, 1 - c, k], fwd_send.at[slot, k], fwd_recv.at[slot, k],
             device_id=(b, mate), device_id_type=MESH)
 
-    for j in range(1, nsamp):
-        hear(j).wait_recv()
-    whole = stats[0]
-    for other in range(1, nsamp):
-        whole = whole + stats[other]
-
     rows_each = width // nsamp
     each = CHUNK // rows_each
     for k in range(nk):
-        part = whole[:, k * CHUNK : (k + 1) * CHUNK]
+        for j in range(1, nsamp):
+            hear(j, k).wait_recv()
+        part = stats[0, k]
+        for other in range(1, nsamp):
+            part = part + stats[other, k]
         cnt, first, second = part[0:1], part[1:2], part[2:3]
         mean = first / cnt
         scale = lax.rsqrt(second - first * mean + eps * cnt)
@@ -264,7 +261,8 @@
     for group in range(ngrp):
         mate_left(group).wait_send()
     for j in range(1, nsamp):
-        tell(j).wait_send()
+        for k in range(nk):
+            tell(j, k).wait_send()
     for k in range(nk):
         for way in (1, 2, 3):
             target, copy = direct(way, k)
@@ -276,6 +274,10 @@
         @pl.when(has(2))
         def _():
             relay(2, b - e, k).wait_send()
+
+
+def hand_on(in_ref, out_ref):
+    out_ref[...] = in_ref[...]
 
 
 def on_device(nblk, nsamp, dosage, observed, band):
@@ -285,7 +287,7 @@
     rows = width // nsamp
     nitems = 5 * nk
     dma = pltpu.SemaphoreType.DMA
-    return pl.pallas_call(
+    linkage = pl.pallas_call(
         functools.partial(linkage_kernel, nblk, nsamp, nk),
         out_shape=jax.ShapeDtypeStruct((rows, 5 * width), jnp.float32),
         in_specs=[
@@ -297,7 +299,7 @@
         scratch_shapes=[
             pltpu.VMEM((nk, depth, CHUNK), jnp.bfloat16),
             pltpu.VMEM((nk, depth, CHUNK), jnp.int32),
-            pltpu.VMEM((nsamp, 8, width), jnp.float32),
+            pltpu.VMEM((nsamp, nk, 8, CHUNK), jnp.float32),
             pltpu.VMEM((5, 2, nk, depth, CHUNK), jnp.bfloat16),
             pltpu.VMEM((2, ngrp, rows, depth), jnp.bfloat16),
             pltpu.VMEM((ngrp, rows, depth), jnp.bfloat16),
@@ -306,8 +308,8 @@
             pltpu.VMEM((nitems, ngrp - 1, rows, CHUNK), jnp.float32),
             dma((nk,)),
             dma((nk,)),
-            dma((nsamp - 1,)),
-            dma((nsamp - 1,)),
+            dma((nsamp - 1, nk)),
+            dma((nsamp - 1, nk)),
             dma((nitems,)),
             dma((4, nk)),
             dma((5, nk)),
@@ -323,6 +325,10 @@
             collective_id=0, has_side_effects=True, vmem_limit_bytes=60 * 1024 * 1024
         ),
     )(band, dosage, observed)
+    block = pl.BlockSpec((rows // 8, 5 * width), lambda i: (i, 0))
+    return pl.pallas_call(
+        hand_on, out_shape=jax.ShapeDtypeStruct(linkage.shape, linkage.dtype), grid=(8,), in_specs=[block], out_specs=block
+    )(linkage)
 
 
 def solution(mesh):

time: 136 us -> 136 us (level)
  local copies, waits for them, and re-layouts: 5.41 us -> 0 us
  Pallas kernels: 130 us -> 135 us
    pallas_call x0 -> x1, Pallas kernels: none -> 7.23 us  [on_device(): pl.pallas_call(hand_on, out_shape=jax.ShapeDtypeStruct(linkage.shape, lin...]
    unnamed x1 -> x0, local copies, waits for them, and re-layouts: 5.41 us -> none
    pallas_call x1, Pallas kernels: 130 us -> 128 us  [on_device(): pl.pallas_call(functools.partial(linkage_kernel, nblk, nsamp, nk), out_sh...]
where the time goes in v5:
time: 136 us; the launch traced here: 135 us
  Pallas kernels  135 us (99%)
    pallas_call x1, Pallas kernels, on_device(): pl.pallas_call(functools.partial(linkage_kernel, nblk, nsamp, nk), out_sh...  128 us
    pallas_call x1, Pallas kernels, on_device(): pl.pallas_call(hand_on, out_shape=jax.ShapeDtypeStruct(linkage.shape, lin...  7.23 us

profile of v5, /device:TPU:12, one launch (start us, length us, event | category | flops | bytes accessed | tf_op | source)
XLA Modules:
  0.0 135.5 jit_solution(7617097621681074921)
XLA Ops:
  0.0 128.3 %shard_map.37.in_ref = f32[256,5120]{1,0:T(8,128)} custom-call(s32[8]{0:T(128)} %band_ref.1, bf16[1280,1024]{1,0:T(8,128)(2,1)} %dosage_ref.1, s32[1280,1024]{1,0:T(8,128)} %observed_ref.1), custom_call_target="tpu_custom_call" | custom-call | tf_op jit(solution)/shard_map/pallas_call | solution.py:290
  128.3 7.2 %shard_map.38 = f32[256,5120]{1,0:T(8,128)} custom-call(f32[256,5120]{1,0:T(8,128)} %shard_map.37.in_ref), custom_call_target="tpu_custom_call" | custom-call | tf_op jit(solution)/shard_map/pallas_call | solution.py:329

commit v6 on v5

--- a/solution.py
+++ b/solution.py
@@ -276,10 +276,6 @@
             relay(2, b - e, k).wait_send()
 
 
-def hand_on(in_ref, out_ref):
-    out_ref[...] = in_ref[...]
-
-
 def on_device(nblk, nsamp, dosage, observed, band):
     depth, width = dosage.shape
     nk = width // CHUNK
@@ -287,7 +283,7 @@
     rows = width // nsamp
     nitems = 5 * nk
     dma = pltpu.SemaphoreType.DMA
-    linkage = pl.pallas_call(
+    return pl.pallas_call(
         functools.partial(linkage_kernel, nblk, nsamp, nk),
         out_shape=jax.ShapeDtypeStruct((rows, 5 * width), jnp.float32),
         in_specs=[
@@ -325,10 +321,6 @@
             collective_id=0, has_side_effects=True, vmem_limit_bytes=60 * 1024 * 1024
         ),
     )(band, dosage, observed)
-    block = pl.BlockSpec((rows // 8, 5 * width), lambda i: (i, 0))
-    return pl.pallas_call(
-        hand_on, out_shape=jax.ShapeDtypeStruct(linkage.shape, linkage.dtype), grid=(8,), in_specs=[block], out_specs=block
-    )(linkage)
 
 
 def solution(mesh):

time: 136 us -> 134 us (0.985)
  Pallas kernels: 135 us -> 128 us
  local copies, waits for them, and re-layouts: 0 us -> 5.41 us
    pallas_call x1 -> x0, Pallas kernels: 7.23 us -> none  [on_device(): pl.pallas_call(hand_on, out_shape=jax.ShapeDtypeStruct(linkage.shape, lin...]
    unnamed x0 -> x1, local copies, waits for them, and re-layouts: none -> 5.41 us
where the time goes in v6:
time: 134 us
  Pallas kernels  128 us (96%)
  local copies, waits for them, and re-layouts  5.41 us (4%)
    pallas_call x1, Pallas kernels, on_device(): pl.pallas_call(functools.partial(linkage_kernel, nblk, nsamp, nk), out_sh...  128 us
    unnamed x1, local copies, waits for them, and re-layouts  5.41 us

profile of v6, /device:TPU:12, one launch (start us, length us, event | category | flops | bytes accessed | tf_op | source)
XLA Modules:
  0.0 133.7 jit_solution(1170242525704028870)
XLA Ops:
  0.0 128.3 %shard_map.37 = f32[256,5120]{1,0:T(8,128)} custom-call(s32[8]{0:T(128)} %band_ref.1, bf16[1280,1024]{1,0:T(8,128)(2,1)} %dosage_ref.1, s32[1280,1024]{1,0:T(8,128)} %observed_ref.1), custom_call_target="tpu_custom_call" | custom-call | tf_op jit(solution)/shard_map/pallas_call | solution.py:286
  128.3 5.4 %copy.5 = f32[256,5120]{1,0:T(8,128)} copy(f32[256,5120]{1,0:T(8,128)} %shard_map.37) | data formatting | bytes 10485760
